TPU v7x, 512 devices: a whole 4x4x16 slice. The times are simulated.
512 devices in a mesh: blk: 32 (over y, x, core), mpo: 16 (over z).
Axes of the slice: x: 4, y: 4, z: 16, core: 2. Of those that a mesh axis runs over, the one named last changes fastest.
Arguments:
- theta: float32 [64, 128, 16, 128], P('blk'), may hold values from -6 to 6
- block_dims: int32 [64, 2], P('blk'), may hold values from 32 to 128, as said below
- pair_mask: int32 [96, 64], P(None, 'blk'), may hold values 0 or 1
- term_charge: int32 [96], replicated, may hold values from -1 to 1
- left_env: float32 [96, 64, 128, 128], P('mpo', 'blk'), may hold values from -0.5 to 0.5
- right_env: float32 [96, 64, 128, 128], P('mpo', 'blk'), may hold values from -0.5 to 0.5
- site_one: float32 [96, 4, 4], replicated, may hold values from -0.3125 to 0.3125
- site_two: float32 [96, 4, 4], replicated, may hold values from -3 to 3
Outputs:
- hpsi: float32 [64, 128, 16, 128], P('blk', 'mpo')
Inputs may be any that keep to these rules, and one draw needn't show every extreme that they name: `block_dims`: kept dimensions of each sector; rows and columns of a block beyond them are empty. The first sector keeps 128 on both sides.
All inputs are finite; a program needn't handle non-finite values. No bound on the sum of `pair_mask` on one device may be relied on, other than what follows from the above.
Results may differ from a plain program's by a relative error of at most 0.0003.
Values sent between devices are 32-bit elements; how exact they have to be, the bound alone decides.
A program may use at most 64 MiB of HBM per device.

v0:
```python
import jax
import jax.numpy as jnp
from jax import lax
from jax.sharding import PartitionSpec as P


def extended(cells, sides, width):
    for axis, dim in sides:
        count = lax.axis_size(axis)
        ends = count - 1
        head = lax.slice_in_dim(cells, 0, width, axis=dim)
        tail = lax.slice_in_dim(cells, cells.shape[dim] - width, cells.shape[dim], axis=dim)
        cells = jnp.concatenate(
            [
                lax.ppermute(tail, axis, [(i, (i + 1) % count) for i in range(ends)]),
                cells,
                lax.ppermute(head, axis, [((i + 1) % count, i) for i in range(ends)]),
            ],
            axis=dim,
        )
    return cells


def sector_mask(block_dims, bond_cap):
    positions = jnp.arange(bond_cap, dtype=jnp.int32)
    left_ok = positions[None, :] < block_dims[:, 0:1]
    right_ok = positions[None, :] < block_dims[:, 1:2]
    return (left_ok[:, :, None] & right_ok[:, None, :]).astype(jnp.float32)


def make_pair(first_op, second_op):
    states = first_op.shape[0]
    return (first_op[:, None, :, None] * second_op[None, :, None, :]).reshape(
        states * states, states * states
    )


def apply_term(left_rows, source, site_pair, right_block):
    highest = lax.Precision.HIGHEST
    row_count = left_rows.shape[0]
    moved = jnp.dot(
        left_rows,
        source.reshape(source.shape[0], -1),
        precision=highest,
        preferred_element_type=jnp.float32,
    )
    moved = moved.reshape(row_count, source.shape[1], source.shape[2])
    mixed = jnp.einsum("pq,aqd->apd", site_pair, moved, precision=highest)
    return jnp.einsum("apd,bd->apb", mixed, right_block, precision=highest)


def all_sectors(running, padded, left_all, right_all, charge, site_pair, allowed):
    sectors = left_all.shape[0]
    source_index = jnp.arange(sectors, dtype=jnp.int32) + 1 - charge

    def per_sector(left_rows, index, right_block):
        source = lax.dynamic_index_in_dim(padded, index, 0, keepdims=False)
        return apply_term(left_rows, source, site_pair, right_block)

    terms = jax.vmap(per_sector)(left_all, source_index, right_all)
    return running + allowed.astype(jnp.float32)[:, None, None, None] * terms


def body(theta, block_dims, pair_mask, term_charge, left_env, right_env, site_one, site_two):
    bond_cap = theta.shape[1]
    group_index = lax.axis_index("mpo")
    group_count = lax.axis_size("mpo")
    row_count = bond_cap // group_count
    first_row = group_index * row_count
    block_mask = sector_mask(block_dims, bond_cap)
    masked = theta * block_mask[:, :, None, :]
    padded = extended(masked, (("blk", 0),), 1)
    row_mask = lax.dynamic_slice_in_dim(block_mask, first_row, row_count, 1)
    term_count = left_env.shape[0]
    first_term = group_index * term_count

    def local_term(w, running):
        term_index = first_term + w
        charge = lax.dynamic_index_in_dim(term_charge, term_index, 0, keepdims=False)
        allowed = lax.dynamic_index_in_dim(pair_mask, term_index, 0, keepdims=False)
        first_op = lax.dynamic_index_in_dim(site_one, term_index, 0, keepdims=False)
        second_op = lax.dynamic_index_in_dim(site_two, term_index, 0, keepdims=False)
        left_all = lax.dynamic_index_in_dim(left_env, w, 0, keepdims=False)
        right_all = lax.dynamic_index_in_dim(right_env, w, 0, keepdims=False)
        return all_sectors(
            running, padded, left_all, right_all, charge, make_pair(first_op, second_op), allowed
        )

    partial_value = lax.fori_loop(0, term_count, local_term, jnp.zeros(theta.shape, jnp.float32))
    whole_sum = lax.psum(partial_value, "mpo")
    mine = lax.dynamic_slice_in_dim(whole_sum, first_row, row_count, 1)
    return mine * row_mask[:, :, None, :]


def solution(mesh):
    placed = (
        P("blk", None, None, None),
        P("blk", None),
        P(None, "blk"),
        P(),
        P("mpo", "blk", None, None),
        P("mpo", "blk", None, None),
        P(),
        P(),
    )
    return jax.shard_map(
        body, mesh=mesh, in_specs=placed, out_specs=P("blk", "mpo", None, None), check_vma=False
    )
```

profile of v0, /device:TPU:2, one launch (start us, length us, event | category | flops | bytes accessed | tf_op | source)
XLA Modules:
  0.0 307.2 jit_solution(4016067030616916532)
XLA Ops:
  13.1 3.6 %collective-permute-start.1 = (f32[1,128,16,128]{3,1,2,0:T(8,128)S(1)}, f32[1,128,16,128]{3,1,2,0:T(8,128)}, u32[]{:S(2)}, u32[]{:S(2)}) collective-permute-start(f32[1,128,16,128]{3,1,2,0:T(8,128)S(1)} %get-tuple-element.253), channel_id=1, source_target_pairs={{16,0},{32,16},{48,32},{64,48},{80,64},{96,80},{112,96},{128,112},... | collective-permute-start | bytes 3145736 | tf_op jit(solution)/shard_map/ppermute | solution.py:17
  17.8 9.7 %collective-permute-done = f32[1,128,16,128]{3,1,2,0:T(8,128)} collective-permute-done((f32[1,128,16,128]{3,1,2,0:T(8,128)}, f32[1,128,16,128]{3,1,2,0:T(8,128)}, u32[]{:S(2)}, u32[]{:S(2)}) %collective-permute-start) | collective-permute-done | bytes 1048608 | tf_op jit(solution)/shard_map/ppermute | solution.py:15
  29.0 4.0 %pad_maximum_fusion = f32[4,128,16,128]{3,1,2,0:T(8,128)} fusion(f32[1,128,16,128]{3,1,2,0:T(8,128)} %collective-permute-done.1, f32[2,128,16,128]{3,1,2,0:T(8,128)S(1)} %copy_multiply_fusion, f32[1,128,16,128]{3,1,2,0:T(8,128)} %collective-permute-done), kind=kLoop, calls=%fused_computation.25 | loop fusion | flops 2097152 | bytes 8388608 | tf_op jit(solution)/shard_map/concatenate | solution.py:13
  33.0 109.8 %while.14 = (s32[]{:T(128)}, f32[2,128,16,128]{3,1,2,0:T(8,128)}, s32[]{:T(128)}, s32[96,2]{1,0:T(8,128)S(1)}, f32[6,2,128,128]{3,2,1,0:T(8,128)}, /*index=5*/s3...) while((s32[]{:T(128)}, f32[2,128,16,128]{3,1,2,0:T(8,128)}, ...), condition=%wide.region_1.2_spmd.clone, body=%wide.region_0.1_spmd.clone.sunk | while | flops 1712849152 | bytes 44307156 | solution.py:89
  35.0 2.9 gather_fusion
  39.7 3.6 %fusion.37 = f32[2,128,2048]{2,1,0:T(8,128)S(1)} fusion(f32[2,128,2048]{1,2,0:T(8,128)} %bitcast.61, f32[6,2,128,128]{3,2,1,0:T(8,128)} %get-tuple-element.351, s32[]{:T(128)S(6)} %copy.41), kind=kOutput, calls=%fused_computation.8.clone.1 | convolution fusion | flops 805306368 | bytes 4325380 | tf_op jit(solution)/shard_map/while/body/eval_jaxpr/vmap()/dot_general | solution.py:41
  45.6 4.4 %select_add_fusion.2 = f32[2,128,16,128]{3,1,2,0:T(8,128)S(1)} fusion(f32[2,128,16,128]{3,1,2,0:T(8,128)S(1)} %copy-done, f32[2,128,128,16]{2,3,1,0:T(8,128)S(1)} %fusion.38, f32[2]{0:T(128)S(1)} %fusion.39, pred[]{:T(512)S(6)} %compare.3, f32[6,2,128,128]{3,2,1,0:T(8,128)} %get-tuple-element.356, s32[]{:T(128)S(6)} %copy.41), kind=kOutput, calls=%fused_computation.6.clone.1 | convolution fusion | flops 806879232 | bytes 6422541 | tf_op jit(solution)/shard_map/while/body/eval_jaxpr/vmap(apd,bd->apb)/dot_general | solution.py:49
  53.3 2.9 gather_fusion
  58.0 3.6 %fusion.37 = f32[2,128,2048]{2,1,0:T(8,128)S(1)} fusion(f32[2,128,2048]{1,2,0:T(8,128)} %bitcast.61, f32[6,2,128,128]{3,2,1,0:T(8,128)} %get-tuple-element.351, s32[]{:T(128)S(6)} %copy.41), kind=kOutput, calls=%fused_computation.8.clone.1 | convolution fusion | flops 805306368 | bytes 4325380 | tf_op jit(solution)/shard_map/while/body/eval_jaxpr/vmap()/dot_general | solution.py:41
  63.9 4.4 %select_add_fusion.2 = f32[2,128,16,128]{3,1,2,0:T(8,128)S(1)} fusion(f32[2,128,16,128]{3,1,2,0:T(8,128)S(1)} %copy-done, f32[2,128,128,16]{2,3,1,0:T(8,128)S(1)} %fusion.38, f32[2]{0:T(128)S(1)} %fusion.39, pred[]{:T(512)S(6)} %compare.3, f32[6,2,128,128]{3,2,1,0:T(8,128)} %get-tuple-element.356, s32[]{:T(128)S(6)} %copy.41), kind=kOutput, calls=%fused_computation.6.clone.1 | convolution fusion | flops 806879232 | bytes 6422541 | tf_op jit(solution)/shard_map/while/body/eval_jaxpr/vmap(apd,bd->apb)/dot_general | solution.py:49
  71.6 2.9 gather_fusion
  76.3 3.6 %fusion.37 = f32[2,128,2048]{2,1,0:T(8,128)S(1)} fusion(f32[2,128,2048]{1,2,0:T(8,128)} %bitcast.61, f32[6,2,128,128]{3,2,1,0:T(8,128)} %get-tuple-element.351, s32[]{:T(128)S(6)} %copy.41), kind=kOutput, calls=%fused_computation.8.clone.1 | convolution fusion | flops 805306368 | bytes 4325380 | tf_op jit(solution)/shard_map/while/body/eval_jaxpr/vmap()/dot_general | solution.py:41
  82.2 4.4 %select_add_fusion.2 = f32[2,128,16,128]{3,1,2,0:T(8,128)S(1)} fusion(f32[2,128,16,128]{3,1,2,0:T(8,128)S(1)} %copy-done, f32[2,128,128,16]{2,3,1,0:T(8,128)S(1)} %fusion.38, f32[2]{0:T(128)S(1)} %fusion.39, pred[]{:T(512)S(6)} %compare.3, f32[6,2,128,128]{3,2,1,0:T(8,128)} %get-tuple-element.356, s32[]{:T(128)S(6)} %copy.41), kind=kOutput, calls=%fused_computation.6.clone.1 | convolution fusion | flops 806879232 | bytes 6422541 | tf_op jit(solution)/shard_map/while/body/eval_jaxpr/vmap(apd,bd->apb)/dot_general | solution.py:49
  89.9 2.9 gather_fusion
  94.6 3.6 %fusion.37 = f32[2,128,2048]{2,1,0:T(8,128)S(1)} fusion(f32[2,128,2048]{1,2,0:T(8,128)} %bitcast.61, f32[6,2,128,128]{3,2,1,0:T(8,128)} %get-tuple-element.351, s32[]{:T(128)S(6)} %copy.41), kind=kOutput, calls=%fused_computation.8.clone.1 | convolution fusion | flops 805306368 | bytes 4325380 | tf_op jit(solution)/shard_map/while/body/eval_jaxpr/vmap()/dot_general | solution.py:41
  100.5 4.4 %select_add_fusion.2 = f32[2,128,16,128]{3,1,2,0:T(8,128)S(1)} fusion(f32[2,128,16,128]{3,1,2,0:T(8,128)S(1)} %copy-done, f32[2,128,128,16]{2,3,1,0:T(8,128)S(1)} %fusion.38, f32[2]{0:T(128)S(1)} %fusion.39, pred[]{:T(512)S(6)} %compare.3, f32[6,2,128,128]{3,2,1,0:T(8,128)} %get-tuple-element.356, s32[]{:T(128)S(6)} %copy.41), kind=kOutput, calls=%fused_computation.6.clone.1 | convolution fusion | flops 806879232 | bytes 6422541 | tf_op jit(solution)/shard_map/while/body/eval_jaxpr/vmap(apd,bd->apb)/dot_general | solution.py:49
  108.2 2.9 gather_fusion
  112.9 3.6 %fusion.37 = f32[2,128,2048]{2,1,0:T(8,128)S(1)} fusion(f32[2,128,2048]{1,2,0:T(8,128)} %bitcast.61, f32[6,2,128,128]{3,2,1,0:T(8,128)} %get-tuple-element.351, s32[]{:T(128)S(6)} %copy.41), kind=kOutput, calls=%fused_computation.8.clone.1 | convolution fusion | flops 805306368 | bytes 4325380 | tf_op jit(solution)/shard_map/while/body/eval_jaxpr/vmap()/dot_general | solution.py:41
  118.8 4.4 %select_add_fusion.2 = f32[2,128,16,128]{3,1,2,0:T(8,128)S(1)} fusion(f32[2,128,16,128]{3,1,2,0:T(8,128)S(1)} %copy-done, f32[2,128,128,16]{2,3,1,0:T(8,128)S(1)} %fusion.38, f32[2]{0:T(128)S(1)} %fusion.39, pred[]{:T(512)S(6)} %compare.3, f32[6,2,128,128]{3,2,1,0:T(8,128)} %get-tuple-element.356, s32[]{:T(128)S(6)} %copy.41), kind=kOutput, calls=%fused_computation.6.clone.1 | convolution fusion | flops 806879232 | bytes 6422541 | tf_op jit(solution)/shard_map/while/body/eval_jaxpr/vmap(apd,bd->apb)/dot_general | solution.py:49
  126.5 2.9 gather_fusion
  131.2 3.6 %fusion.37 = f32[2,128,2048]{2,1,0:T(8,128)S(1)} fusion(f32[2,128,2048]{1,2,0:T(8,128)} %bitcast.61, f32[6,2,128,128]{3,2,1,0:T(8,128)} %get-tuple-element.351, s32[]{:T(128)S(6)} %copy.41), kind=kOutput, calls=%fused_computation.8.clone.1 | convolution fusion | flops 805306368 | bytes 4325380 | tf_op jit(solution)/shard_map/while/body/eval_jaxpr/vmap()/dot_general | solution.py:41
  137.1 4.4 %select_add_fusion.2 = f32[2,128,16,128]{3,1,2,0:T(8,128)S(1)} fusion(f32[2,128,16,128]{3,1,2,0:T(8,128)S(1)} %copy-done, f32[2,128,128,16]{2,3,1,0:T(8,128)S(1)} %fusion.38, f32[2]{0:T(128)S(1)} %fusion.39, pred[]{:T(512)S(6)} %compare.3, f32[6,2,128,128]{3,2,1,0:T(8,128)} %get-tuple-element.356, s32[]{:T(128)S(6)} %copy.41), kind=kOutput, calls=%fused_computation.6.clone.1 | convolution fusion | flops 806879232 | bytes 6422541 | tf_op jit(solution)/shard_map/while/body/eval_jaxpr/vmap(apd,bd->apb)/dot_general | solution.py:49
  142.8 4.2 %copy.20 = f32[2,128,16,128]{3,2,1,0:T(8,128)} copy(f32[2,128,16,128]{3,1,2,0:T(8,128)} %get-tuple-element.174) | data formatting | bytes 4194304 | tf_op jit(solution)/shard_map/while | solution.py:89
  147.0 151.8 %all-reduce.2.cloned.1.call-done = f32[2,128,16,128]{3,2,1,0:T(8,128)} async-done(((f32[2,128,16,128]{3,2,1,0:T(8,128)}), f32[2,128,16,128]{3,2,1,0:T(8,128)}) %all-reduce.2.cloned.1.call-update) | async-done | bytes 2097168 | tf_op jit(solution)/shard_map/psum | solution.py:90
  (101 shorter events, 55.1 us)
Async XLA Ops:
  6.5 292.3 %all-reduce.2.cloned.1.call-start = ((), (), s32[]{:S(2)}) async-start(), calls=%async_computation | async-start | bytes 4194304 | tf_op jit(solution)/shard_map/psum | solution.py:90
  9.9 6.8 %copy-start.4 = (s32[96,2]{0,1:T(2,128)S(1)}, s32[96,2]{0,1:T(2,128)}, u32[]{:S(2)}) copy-start(s32[96,2]{0,1:T(2,128)} %param.12) | copy-start | bytes 2308
  10.0 6.9 %copy-start.2 = (f32[96,4,4]{0,2,1:T(4,128)S(1)}, f32[96,4,4]{0,2,1:T(4,128)}, u32[]{:S(2)}) copy-start(f32[96,4,4]{0,2,1:T(4,128)} %param.16) | copy-start | bytes 18436
  10.0 7.0 %copy-start.3 = (f32[96,4,4]{0,2,1:T(4,128)S(1)}, f32[96,4,4]{0,2,1:T(4,128)}, u32[]{:S(2)}) copy-start(f32[96,4,4]{0,2,1:T(4,128)} %param.17) | copy-start | bytes 18436
  11.1 16.4 %collective-permute-start = (f32[1,128,16,128]{3,1,2,0:T(8,128)}, f32[1,128,16,128]{3,1,2,0:T(8,128)}, u32[]{:S(2)}, u32[]{:S(2)}) collective-permute-start(f32[1,128,16,128]{3,1,2,0:T(8,128)} %get-tuple-element.252), channel_id=1, source_target_pairs={{0,16},{16,32},{32,48},{48,64},{64,80},{80,96},{96,112},{112,128},... | collective-permute-start | bytes 3145736 | tf_op jit(solution)/shard_map/ppermute | solution.py:15
  13.1 15.9 %collective-permute-start.1 = (f32[1,128,16,128]{3,1,2,0:T(8,128)S(1)}, f32[1,128,16,128]{3,1,2,0:T(8,128)}, u32[]{:S(2)}, u32[]{:S(2)}) collective-permute-start(f32[1,128,16,128]{3,1,2,0:T(8,128)S(1)} %get-tuple-element.253), channel_id=1, source_target_pairs={{16,0},{32,16},{48,32},{64,48},{80,64},{96,80},{112,96},{128,112},... | collective-permute-start | bytes 3145736 | tf_op jit(solution)/shard_map/ppermute | solution.py:17
  17.8 15.1 %copy-start.5 = (s32[96]{0:T(128)S(1)}, s32[96]{0:T(128)}, u32[]{:S(2)}) copy-start(s32[96]{0:T(128)} %param.13) | copy-start | bytes 1156
  43.7 1.9 copy-start
  49.9 1.3 copy-start.1
  62.0 1.9 copy-start
  68.3 1.3 copy-start.1
  80.3 1.9 copy-start
  86.6 1.3 copy-start.1
  98.6 1.9 copy-start
  104.9 1.3 copy-start.1
  116.9 1.9 copy-start
  123.2 1.3 copy-start.1
  135.2 1.9 copy-start
  141.5 1.3 copy-start.1
Sparse Core Ops, SparseCore 0:
  147.1 151.6 all-reduce.1
where the time goes:
time: 308 us; the launch traced here: 307 us
  waiting for transfers between devices  163 us (53%)
  matrix products  58.9 us (19%)
  local copies, waits for them, and re-layouts  53.9 us (18%)
  between operations  13.5 us (4%)
  other arithmetic  11.8 us (4%)
  starting transfers between devices  5.55 us (2%)
    psum x1, waiting for transfers between devices, body(): whole_sum = lax.psum(partial_value, 'mpo')  152 us
    gather x12, local copies, waits for them, and re-layouts, per_sector(): source = lax.dynamic_index_in_dim(padded, index, 0, keepdims=False)  28.4 us
    dot_general x6, matrix products, apply_term(): return jnp.einsum('apd,bd->apb', mixed, right_block, precision=highest)  26.2 us
    dot_general x6, matrix products, apply_term(): jnp.dot(left_rows, source.reshape(source.shape[0], -1), precision=highest...  21.4 us
    dot_general x6, matrix products, apply_term(): mixed = jnp.einsum('pq,aqd->apd', site_pair, moved, precision=highest)  11.3 us
    while x30, local copies, waits for them, and re-layouts  10.3 us
    ppermute x1, waiting for transfers between devices, extended(): lax.ppermute(tail, axis, [(i, (i + 1) % count) for i in range(ends)])  9.72 us
  transfers between devices with their start and end apart: 3, of which 3 were waited for; matrix products, arithmetic and copies ran while one was open for 0% of the time, Pallas kernels for 0%

commit v1 on v0

--- a/solution.py
+++ b/solution.py
@@ -87,7 +87,8 @@
         )
 
     partial_value = lax.fori_loop(0, term_count, local_term, jnp.zeros(theta.shape, jnp.float32))
-    whole_sum = lax.psum(partial_value, "mpo")
+    shards = lax.all_gather(partial_value, "mpo", axis=0, tiled=False)
+    whole_sum = shards.sum(axis=0)
     mine = lax.dynamic_slice_in_dim(whole_sum, first_row, row_count, 1)
     return mine * row_mask[:, :, None, :]
 

time: 308 us -> 535 us (1.74)
  the two profiles are of different devices: /device:TPU:2 before, /device:TPU:1 now
where the time goes in v1:
time: 535 us; the launch traced here: 534 us
  waiting for transfers between devices  373 us (70%)
  matrix products  59.1 us (11%)
  local copies, waits for them, and re-layouts  54.6 us (10%)
  other arithmetic  22.3 us (4%)
  between operations  13.5 us (3%)
  starting transfers between devices  11 us (2%)
    all_gather x1, waiting for transfers between devices, body(): shards = lax.all_gather(partial_value, 'mpo', axis=0, tiled=False)  364 us
    gather x12, local copies, waits for them, and re-layouts, per_sector(): source = lax.dynamic_index_in_dim(padded, index, 0, keepdims=False)  28.4 us
    dot_general x6, matrix products, apply_term(): return jnp.einsum('apd,bd->apb', mixed, right_block, precision=highest)  26.2 us
    dot_general x6, matrix products, apply_term(): jnp.dot(left_rows, source.reshape(source.shape[0], -1), precision=highest...  21.4 us
    reduce_sum x1, other arithmetic, body(): whole_sum = shards.sum(axis=0)  12.1 us
    dot_general x6, matrix products, apply_term(): mixed = jnp.einsum('pq,aqd->apd', site_pair, moved, precision=highest)  11.5 us
  transfers between devices with their start and end apart: 3, of which 3 were waited for; matrix products, arithmetic and copies ran while one was open for 0% of the time, Pallas kernels for 0%

profile of v1, /device:TPU:1, one launch (start us, length us, event | category | flops | bytes accessed | tf_op | source)
XLA Modules:
  0.0 533.7 jit_solution(6946920197046462683)
XLA Ops:
  11.1 4.5 collective-permute-start
  15.6 6.5 %collective-permute-start.1 = (f32[1,128,16,128]{3,1,2,0:T(8,128)S(1)}, f32[1,128,16,128]{3,1,2,0:T(8,128)}, u32[]{:S(2)}, u32[]{:S(2)}) collective-permute-start(f32[1,128,16,128]{3,1,2,0:T(8,128)S(1)} %get-tuple-element.263), channel_id=1, source_target_pairs={{16,0},{32,16},{48,32},{64,48},{80,64},{96,80},{112,96},{128,112},... | collective-permute-start | bytes 3145736 | tf_op jit(solution)/shard_map/ppermute | solution.py:17
  23.3 4.4 collective-permute-done
  27.7 4.2 collective-permute-done.1
  31.9 3.9 pad_maximum_fusion
  35.7 110.0 %while.14 = (s32[]{:T(128)}, f32[2,128,16,128]{3,1,2,0:T(8,128)}, s32[]{:T(128)}, s32[96,2]{1,0:T(8,128)S(1)}, f32[6,2,128,128]{3,2,1,0:T(8,128)}, /*index=5*/s3...) while((s32[]{:T(128)}, f32[2,128,16,128]{3,1,2,0:T(8,128)}, ...), condition=%wide.region_1.2_spmd.clone, body=%wide.region_0.1_spmd.clone.sunk | while | flops 1712849152 | bytes 44307156 | solution.py:89
  42.4 3.6 fusion.39
  48.3 4.4 select_add_fusion.2
  56.0 2.9 gather_fusion
  60.8 3.6 fusion.39
  66.7 4.4 select_add_fusion.2
  74.4 2.9 gather_fusion
  79.1 3.6 fusion.39
  85.0 4.4 select_add_fusion.2
  92.7 2.9 gather_fusion
  97.4 3.6 fusion.39
  103.4 4.4 select_add_fusion.2
  115.8 3.6 fusion.39
  121.7 4.4 select_add_fusion.2
  134.1 3.6 fusion.39
  140.0 4.4 select_add_fusion.2
  145.7 4.1 copy.26
  149.9 364.0 %all-gather.3.cloned.1.call-done = f32[32,128,16,128]{3,2,1,0:T(8,128)} async-done(((f32[2,128,16,128]{3,2,1,0:T(8,128)}), f32[32,128,16,128]{3,2,1,0:T(8,128)}) %all-gather.3.cloned.1.call-update) | async-done | bytes 33554448 | tf_op jit(solution)/shard_map/all_gather | solution.py:90
  514.0 12.1 %reduce_sum.9 = f32[2,128,16,128]{3,2,1,0:T(8,128)S(1)} reduce(f32[16,2,128,16,128]{4,3,2,1,0:T(8,128)} %bitcast.63, f32[]{:T(128)} %constant.69.clone.1), dimensions={0}, to_apply=%region_2.3 | reduce | flops 7864320 | bytes 35651588 | tf_op jit(solution)/shard_map/reduce_sum | solution.py:91
  (104 shorter events, 59.7 us)
Async XLA Ops:
  6.5 507.4 %all-gather.3.cloned.1.call-start = ((), (), s32[]{:S(2)}) async-start(), calls=%async_computation | async-start | bytes 35651584 | tf_op jit(solution)/shard_map/all_gather | solution.py:90
  9.9 12.2 %copy-start.4 = (s32[96,2]{0,1:T(2,128)S(1)}, s32[96,2]{0,1:T(2,128)}, u32[]{:S(2)}) copy-start(s32[96,2]{0,1:T(2,128)} %param.12) | copy-start | bytes 2308
  10.0 12.3 %copy-start.2 = (f32[96,4,4]{0,2,1:T(4,128)S(1)}, f32[96,4,4]{0,2,1:T(4,128)}, u32[]{:S(2)}) copy-start(f32[96,4,4]{0,2,1:T(4,128)} %param.16) | copy-start | bytes 18436
  10.0 12.5 %copy-start.3 = (f32[96,4,4]{0,2,1:T(4,128)S(1)}, f32[96,4,4]{0,2,1:T(4,128)}, u32[]{:S(2)}) copy-start(f32[96,4,4]{0,2,1:T(4,128)} %param.17) | copy-start | bytes 18436
  11.1 16.5 %collective-permute-start = (f32[1,128,16,128]{3,1,2,0:T(8,128)}, f32[1,128,16,128]{3,1,2,0:T(8,128)}, u32[]{:S(2)}, u32[]{:S(2)}) collective-permute-start(f32[1,128,16,128]{3,1,2,0:T(8,128)} %get-tuple-element.262), channel_id=1, source_target_pairs={{0,16},{16,32},{32,48},{48,64},{64,80},{80,96},{96,112},{112,128},... | collective-permute-start | bytes 3145736 | tf_op jit(solution)/shard_map/ppermute | solution.py:15
  15.6 16.2 %collective-permute-start.1 = (f32[1,128,16,128]{3,1,2,0:T(8,128)S(1)}, f32[1,128,16,128]{3,1,2,0:T(8,128)}, u32[]{:S(2)}, u32[]{:S(2)}) collective-permute-start(f32[1,128,16,128]{3,1,2,0:T(8,128)S(1)} %get-tuple-element.263), channel_id=1, source_target_pairs={{16,0},{32,16},{48,32},{64,48},{80,64},{96,80},{112,96},{128,112},... | collective-permute-start | bytes 3145736 | tf_op jit(solution)/shard_map/ppermute | solution.py:17
  23.3 12.4 %copy-start.5 = (s32[96]{0:T(128)S(1)}, s32[96]{0:T(128)}, u32[]{:S(2)}) copy-start(s32[96]{0:T(128)} %param.13) | copy-start | bytes 1156
  46.4 1.9 copy-start
  52.7 1.3 copy-start.1
  64.7 1.9 copy-start
  71.1 1.3 copy-start.1
  83.1 1.9 copy-start
  89.4 1.3 copy-start.1
  101.4 1.9 copy-start
  107.7 1.3 copy-start.1
  119.8 1.9 copy-start
  126.1 1.3 copy-start.1
  138.1 1.9 copy-start
  144.4 1.3 copy-start.1
Sparse Core Ops, SparseCore 0:
  150.0 363.8 all-gather.2
